TPU v7x, 256 devices: a whole 4x4x8 slice. The times are simulated.
256 devices in a mesh: dp: 8 (over y, z_hi), expert: 32 (over z_lo, x, core).
Axes of the slice: x: 4, y: 4, z: 8 (z_hi: 2, z_lo: 4; z = z_hi * 4 + z_lo), core: 2. Of those that a mesh axis runs over, the one named last changes fastest.
Arguments:
- activations: bfloat16 [32768, 4096], P(('dp', 'expert')), may hold values from -6 to 6
- cotangent: bfloat16 [32768, 4096], P(('dp', 'expert')), may hold values from -6 to 6
- expert_ids: int32 [32768, 1], P(('dp', 'expert')), may hold values from 0 to 127; in each aligned block of 128 rows (0 to 127, 128 to 255, ...) at most 2 rows name the same one
- gate_probs: float32 [32768, 1], P(('dp', 'expert')), may hold values from 0.2 to 1
- gate_up: bfloat16 [32, 2, 4096, 1536], P('expert', None, None, 'dp'), may hold values from -0.09375 to 0.09375
- down_proj: bfloat16 [32, 1536, 4096], P('expert', 'dp'), may hold values from -0.15625 to 0.15625
Outputs:
- input_grad: bfloat16 [32768, 4096], P(('dp', 'expert'))
- grad_gate_up: bfloat16 [32, 2, 4096, 1536], P('expert', None, None, 'dp')
- grad_down: bfloat16 [32, 1536, 4096], P('expert', 'dp')
Inputs may be any that keep to these rules, and one draw needn't show every extreme that they name: `expert_ids`: expert e < 32 is held by index e of the expert axis. Among the 128 tokens of one device no expert is named more than 2 times, a bound that some block reaches.
All inputs are finite; a program needn't handle non-finite values.
Results may differ from a plain program's by a relative error of at most 0.0058.
Values may be sent and summed in bfloat16 or wider, within the bound.
A program may use at most 128 MiB of HBM per device.

v0:
```python
import jax
import jax.numpy as jnp
from jax import lax
from jax.sharding import PartitionSpec as P

CAP = 2


def contract(left, right, left_dim, right_dim):
    return lax.dot_general(
        left, right, (((left_dim,), (right_dim,)), ((), ())), preferred_element_type=jnp.float32
    )


def block_backward(rows_tok, rows_cot, pair_weights, down_weights):
    pre_gate = jnp.dot(rows_tok, pair_weights[0], preferred_element_type=jnp.float32)
    pre_up = jnp.dot(rows_tok, pair_weights[1], preferred_element_type=jnp.float32)
    sigmoid_gate = jax.nn.sigmoid(pre_gate)
    activated = pre_gate * sigmoid_gate
    hidden = (activated * pre_up).astype(jnp.bfloat16)
    hidden_grad = contract(rows_cot, down_weights, 1, 1)
    gate_grad = (
        hidden_grad * pre_up * sigmoid_gate * (1.0 + pre_gate * (1.0 - sigmoid_gate))
    ).astype(jnp.bfloat16)
    up_grad = (hidden_grad * activated).astype(jnp.bfloat16)
    total_down = contract(hidden, rows_cot, 0, 0)
    total_gate = contract(rows_tok, gate_grad, 0, 0)
    total_up = contract(rows_tok, up_grad, 0, 0)
    input_rows = contract(gate_grad, pair_weights[0], 1, 1) + contract(
        up_grad, pair_weights[1], 1, 1
    )
    return (total_gate, total_up, total_down, input_rows)


def expert_rows(rows_tok, rows_cot, pair_weights, down_weights):
    row_count = rows_tok.shape[0]
    block_rows = min(256, row_count)
    model_width = rows_tok.shape[1]
    unit_count = down_weights.shape[0]
    alive_flag = jnp.any(rows_cot != 0, axis=1).astype(jnp.int32)
    ordering = jnp.argsort(1 - alive_flag, stable=True)
    live_count = jnp.sum(alive_flag)
    block_count = (live_count + block_rows - 1) // block_rows

    def advance(counter, carry_state):
        total_gate, total_up, total_down, input_all = carry_state
        picked = lax.dynamic_slice_in_dim(ordering, counter * block_rows, block_rows)
        part_tok = jnp.take(rows_tok, picked, axis=0)
        part_cot = jnp.take(rows_cot, picked, axis=0)
        more_gate, more_up, more_down, input_rows = block_backward(
            part_tok, part_cot, pair_weights, down_weights
        )
        input_all = input_all.at[picked].set(input_rows)
        return (total_gate + more_gate, total_up + more_up, total_down + more_down, input_all)

    initial = (
        jnp.zeros((model_width, unit_count), jnp.float32),
        jnp.zeros((model_width, unit_count), jnp.float32),
        jnp.zeros((unit_count, model_width), jnp.float32),
        jnp.zeros((row_count, model_width), jnp.float32),
    )
    total_gate, total_up, total_down, input_all = lax.fori_loop(0, block_count, advance, initial)
    return (jnp.stack([total_gate, total_up]), total_down, input_all)


def per_device(activations, cotangent, expert_ids, gate_probs, gate_up, down_proj):
    experts = lax.axis_size("expert")
    identity = expert_ids[:, 0]
    in_window = identity < experts
    onehot = (identity[:, None] == jnp.arange(experts, dtype=jnp.int32)[None, :]).astype(jnp.int32)
    before = jnp.cumsum(onehot, axis=0) - onehot
    ranking = jnp.sum(before * onehot, axis=1)
    slot_index = identity * CAP + ranking
    slot_index = jnp.where(in_window, slot_index, -1)
    placing = (slot_index[None, :] == jnp.arange(experts * CAP, dtype=jnp.int32)[:, None]).astype(
        jnp.bfloat16
    )
    scaled = (gate_probs * cotangent.astype(jnp.float32)).astype(jnp.bfloat16)
    send_tok = jnp.dot(placing, activations, preferred_element_type=jnp.float32).astype(
        jnp.bfloat16
    )
    send_cot = jnp.dot(placing, scaled, preferred_element_type=jnp.float32).astype(jnp.bfloat16)
    got_tok, got_cot = (
        lax.all_to_all(send_tok, "expert", split_axis=0, concat_axis=0, tiled=True),
        lax.all_to_all(send_cot, "expert", split_axis=0, concat_axis=0, tiled=True),
    )
    all_tok, all_cot = (
        lax.all_gather(got_tok, "dp", axis=0, tiled=True),
        lax.all_gather(got_cot, "dp", axis=0, tiled=True),
    )
    own_pair = gate_up[0]
    own_down = down_proj[0]
    pair_total, down_total, partial_value = expert_rows(all_tok, all_cot, own_pair, own_down)
    summed = lax.psum_scatter(partial_value, "dp", scatter_dimension=0, tiled=True)
    rounded = summed.astype(jnp.bfloat16)
    returned = lax.all_to_all(rounded, "expert", split_axis=0, concat_axis=0, tiled=True)
    input_grad = contract(placing, returned, 0, 0).astype(jnp.bfloat16)
    return (
        input_grad,
        pair_total[None].astype(jnp.bfloat16),
        down_total[None].astype(jnp.bfloat16),
    )


def solution(mesh):
    in_specs = (
        P(("dp", "expert"), None),
        P(("dp", "expert"), None),
        P(("dp", "expert"), None),
        P(("dp", "expert"), None),
        P("expert", None, None, "dp"),
        P("expert", "dp", None),
    )
    out_specs = (P(("dp", "expert"), None), P("expert", None, None, "dp"), P("expert", "dp", None))
    return jax.shard_map(
        per_device, mesh=mesh, in_specs=in_specs, out_specs=out_specs, check_vma=False
    )
```

profile of v0, /device:TPU:1, one launch (start us, length us, event | category | flops | bytes accessed | tf_op | source)
XLA Modules:
  0.0 565.2 jit_solution(4953973455181101589)
XLA Ops:
  7.2 0.0 copy-start
  7.2 0.0 all-gather.3.cloned.1.call-start
  7.2 0.8 fusion.18
  8.0 0.2 reduce_window_sum.11
  8.2 0.8 select_reduce_fusion
  9.1 0.7 compare_select_fusion.1
  9.7 1.6 convolution_convert_fusion.2
  11.4 0.3 all_to_all.24
  11.7 26.2 %all_to_all.36 = bf16[32,2,4096]{2,1,0:T(2,128)(2,1)S(1)} all-to-all(bf16[32,2,4096]{2,1,0:T(2,128)(2,1)S(1)} %all_to_all.24), channel_id=1, replica_groups=mesh['dp'=8,'expert'=32] {'expert'}, dimensions={0} | all-to-all | bytes 1048576 | tf_op jit(solution)/shard_map/all_to_all | solution.py:85
  37.9 1.0 all_to_all.26
  38.9 0.0 all-gather.3.cloned.1.call-update
  38.9 0.0 all-gather.5.cloned.1.call-start
  39.0 0.0 copy-done
  39.0 0.3 convolution_convert_fusion.1
  39.3 0.0 copy-done.8
  39.3 0.3 all_to_all.27
  39.7 31.5 %all_to_all.37 = bf16[32,2,4096]{2,1,0:T(2,128)(2,1)S(1)} all-to-all(bf16[32,2,4096]{2,1,0:T(2,128)(2,1)S(1)} %all_to_all.27), channel_id=1, replica_groups=mesh['dp'=8,'expert'=32] {'expert'}, dimensions={0} | all-to-all | bytes 1048576 | tf_op jit(solution)/shard_map/all_to_all | solution.py:84
  71.2 1.0 all_to_all.29
  72.2 0.0 all-gather.5.cloned.1.call-update
  72.2 0.0 reduce-scatter.2.cloned.1.call-start
  72.3 6.1 %copy.9 = bf16[1,2,4096,192]{3,2,1,0:T(8,128)(2,1)} copy(bf16[1,2,4096,192]{2,3,1,0:T(8,128)(2,1)} %param.14) | data formatting | bytes 6291456 | tf_op args[4]
  78.3 68.2 %all-gather.3.cloned.1.call-done = bf16[512,4096]{1,0:T(8,128)(2,1)} async-done(((bf16[64,4096]{1,0:T(8,128)(2,1)}), bf16[512,4096]{1,0:T(8,128)(2,1)}) %all-gather.3.cloned.1.call-update) | async-done | bytes 4194320 | tf_op jit(solution)/shard_map/all_gather | solution.py:89
  146.5 3.3 compare_reduce_fusion
  149.9 0.6 convert_subtract_fusion
  151.2 3.8 sort.17
  154.9 96.6 %all-gather.5.cloned.1.call-done = bf16[512,4096]{1,0:T(8,128)(2,1)} async-done(((bf16[64,4096]{1,0:T(8,128)(2,1)}), bf16[512,4096]{1,0:T(8,128)(2,1)}) %all-gather.5.cloned.1.call-update) | async-done | bytes 4194320 | tf_op jit(solution)/shard_map/all_gather | solution.py:88
  251.5 2.1 broadcast.32.clone
  253.6 2.1 broadcast_in_dim.28
  255.7 2.0 broadcast.32
  257.7 4.2 broadcast_in_dim.29
  262.0 46.4 %while.16 = (s32[]{:T(128)}, f32[4096,192]{0,1:T(8,128)}, f32[4096,192]{0,1:T(8,128)}, f32[192,4096]{1,0:T(8,128)}, f32[512,4096]{1,0:T(8,128)}, /*index=5*/s32[...) while((s32[]{:T(128)}, f32[4096,192]{0,1:T(8,128)}, ...), condition=%wide.region_7.9_spmd, body=%wide.region_5.8_spmd.sunk | while | flops 3231861248 | bytes 160641424 | solution.py:62
  262.0 0.1 compare_and_fusion.2
  262.1 6.6 %gather_fusion = bf16[256,4096]{1,0:T(8,128)(2,1)S(1)} fusion(bf16[512,4096]{1,0:T(8,128)(2,1)} %get-tuple-element.214, s32[1024]{0:T(1024)S(1)} %pad_clamp_fusion.2), kind=kCustom, calls=%fused_computation.clone.clone.1 | custom fusion | bytes 4195328 | tf_op jit(solution)/shard_map/while/body/jit(_take)/gather | solution.py:48
  268.7 0.0 copy-start.6
  268.7 2.8 fusion.51
  271.5 0.0 copy-done.6
  271.5 1.1 fusion.50
  272.6 7.9 %gather_fusion.1 = bf16[256,4096]{1,0:T(8,128)(2,1)} fusion(bf16[512,4096]{1,0:T(8,128)(2,1)} %get-tuple-element.215, s32[1024]{0:T(1024)S(1)} %pad_clamp_fusion.2), kind=kCustom, calls=%fused_computation.1.clone.clone.1 | custom fusion | bytes 4195328 | tf_op jit(solution)/shard_map/while/body/jit(_take)/gather | solution.py:49
  280.6 3.1 multiply_convert_fusion.9
  283.7 0.0 copy-done.1
  283.7 0.0 copy-start.4
  283.7 4.5 convolution_add_fusion.10
  288.2 0.0 copy-done.4
  288.2 0.9 convolution_add_fusion.8
  289.1 0.0 copy-start.5
  289.1 1.7 copy-done.5
  290.8 0.0 copy-done.2
  290.8 0.9 convolution_add_fusion.9
  291.7 1.7 copy-done.3
  293.5 0.3 copy-done.7
  293.8 0.8 fusion.52
  294.6 2.7 convolution_add_fusion.11
  297.3 11.1 %scatter_fusion = f32[512,4096]{1,0:T(8,128)} fusion(f32[512,4096]{1,0:T(8,128)} %get-tuple-element.196, s32[256]{0:T(256)S(1)} %get-tuple-element.173, f32[256,4096]{1,0:T(8,128)} %convolution_add_fusion.11), kind=kCustom, calls=%fused_computation.2.clone.1 | custom fusion | bytes 12583936 | tf_op jit(solution)/shard_map/while/body/scatter | solution.py:53
  308.4 0.0 reduce-scatter.2.cloned.1.call-update
  308.4 4.4 convert_bitcast_fusion.1
  312.9 217.2 %reduce-scatter.2.cloned.1.call-done = f32[64,4096]{1,0:T(8,128)} async-done(((f32[512,4096]{1,0:T(8,128)}), f32[64,4096]{1,0:T(8,128)}) %reduce-scatter.2.cloned.1.call-update) | async-done | bytes 1048592 | tf_op jit(solution)/shard_map/reduce_scatter | solution.py:94
  530.1 1.3 convert_element_type.55
  531.4 1.1 all_to_all.30
  532.5 8.1 %all-to-all-start.2 = ((bf16[32,2,4096]{2,1,0:T(2,128)(2,1)}), bf16[32,2,4096]{2,1,0:T(2,128)(2,1)S(1)}, u32[]{:S(2)}, u32[]{:S(2)}) async-start(bf16[32,2,4096]{2,1,0:T(2,128)(2,1)} %all_to_all.30), calls=%async_computation.3 | async-start | bytes 1048576 | tf_op jit(solution)/shard_map/all_to_all | solution.py:96
  540.6 3.4 pad_maximum_fusion
  544.0 3.2 convert_bitcast_fusion
  547.2 9.8 %all-to-all-done.2 = bf16[32,2,4096]{2,1,0:T(2,128)(2,1)S(1)} async-done(((bf16[32,2,4096]{2,1,0:T(2,128)(2,1)}), bf16[32,2,4096]{2,1,0:T(2,128)(2,1)S(1)}, u32[]{:S(2)}, u32[]{:S(2)}) %all-to-all-start.2) | async-done | bytes 524320 | tf_op jit(solution)/shard_map/all_to_all | solution.py:96
  557.1 0.2 all_to_all.32
  557.3 1.5 convolution_convert_fusion
  (9 shorter events, 0.0 us)
Async XLA Ops:
  7.2 31.8 %copy-start = (bf16[128,4096]{1,0:T(8,128)(2,1)S(1)}, bf16[128,4096]{1,0:T(8,128)(2,1)}, u32[]{:S(2)}) copy-start(bf16[128,4096]{1,0:T(8,128)(2,1)} %param.10) | copy-start | bytes 3145732
  7.2 139.4 %all-gather.3.cloned.1.call-start = ((), (), s32[]{:S(2)}) async-start(), calls=%async_computation.4 | async-start | bytes 4718592 | tf_op jit(solution)/shard_map/all_gather | solution.py:89
  9.7 29.6 %copy-start.8 = (s32[128]{0:T(128)}, s32[128]{0:T(128)S(1)}, u32[]{:S(2)}) copy-start(s32[128]{0:T(128)S(1)} %compare_select_fusion.1) | copy-start | bytes 1540
  38.9 212.6 %all-gather.5.cloned.1.call-start = ((), (), s32[]{:S(2)}) async-start(), calls=%async_computation.5 | async-start | bytes 4718592 | tf_op jit(solution)/shard_map/all_gather | solution.py:88
  72.2 457.9 %reduce-scatter.2.cloned.1.call-start = ((), (), s32[]{:S(2)}) async-start(), calls=%async_computation.6 | async-start | bytes 9437184 | tf_op jit(solution)/shard_map/reduce_scatter | solution.py:94
  268.7 2.8 copy-start.6
  280.6 3.1 copy-start.1
  283.7 4.5 copy-start.4
  288.2 2.6 copy-start.2
  289.1 1.7 copy-start.5
  290.8 3.0 copy-start.7
  291.7 1.8 copy-start.3
  532.5 24.6 %all-to-all-start.2 = ((bf16[32,2,4096]{2,1,0:T(2,128)(2,1)}), bf16[32,2,4096]{2,1,0:T(2,128)(2,1)S(1)}, u32[]{:S(2)}, u32[]{:S(2)}) async-start(bf16[32,2,4096]{2,1,0:T(2,128)(2,1)} %all_to_all.30), calls=%async_computation.3 | async-start | bytes 1048576 | tf_op jit(solution)/shard_map/all_to_all | solution.py:96
  544.0 13.3 %copy-start.9 = (s32[128]{0:T(128)S(1)}, s32[128]{0:T(128)}, u32[]{:S(2)}) copy-start(s32[128]{0:T(128)} %copy-done.8) | copy-start | bytes 1540
Sparse Core Ops, SparseCore 0:
  39.1 107.4 all-gather.2
  149.7 101.7 all-gather.4
  308.5 221.5 reduce-scatter.1
where the time goes:
time: 566 us; the launch traced here: 565 us
  waiting for transfers between devices  392 us (69%)
  blocking collectives  57.8 us (10%)
  local copies, waits for them, and re-layouts  49.9 us (9%)
  other arithmetic  22.6 us (4%)
  matrix products  20.2 us (4%)
  between operations  14.5 us (3%)
  starting transfers between devices  8.24 us (1%)
    reduce_scatter x1, waiting for transfers between devices, per_device(): lax.psum_scatter(partial_value, 'dp', scatter_dimension=0, tiled=True)  217 us
    all_gather x1, waiting for transfers between devices, per_device(): lax.all_gather(got_tok, 'dp', axis=0, tiled=True)  96.6 us
    all_gather x1, waiting for transfers between devices, per_device(): lax.all_gather(got_cot, 'dp', axis=0, tiled=True)  68.2 us
    all_to_all x1, blocking collectives, per_device(): lax.all_to_all(send_tok, 'expert', split_axis=0, concat_axis=0, tiled=True)  31.5 us
    all_to_all x1, blocking collectives, per_device(): lax.all_to_all(send_cot, 'expert', split_axis=0, concat_axis=0, tiled=True)  26.2 us
    dot_general x7, matrix products, contract(): lax.dot_general(left, right, (((left_dim,), (right_dim,)), ((), ())), pre...  14.4 us
  transfers between devices with their start and end apart: 4, of which 4 were waited for; matrix products, arithmetic and copies ran while one was open for 4% of the time, Pallas kernels for 0%

commit v1 on v0

--- a/solution.py
+++ b/solution.py
@@ -4,6 +4,11 @@
 from jax.sharding import PartitionSpec as P
 
 CAP = 2
+
+
+def gather_over(x, axis, dim):
+    stack = jnp.stack([x] * lax.axis_size(axis))
+    return jnp.concatenate(lax.all_to_all(stack, axis, 0, 0), axis=dim)
 
 
 def contract(left, right, left_dim, right_dim):
@@ -85,7 +90,7 @@
         lax.all_to_all(send_cot, "expert", split_axis=0, concat_axis=0, tiled=True),
     )
     all_tok, all_cot = (
-        lax.all_gather(got_tok, "dp", axis=0, tiled=True),
+        gather_over(got_tok, "dp", 0),
         lax.all_gather(got_cot, "dp", axis=0, tiled=True),
     )
     own_pair = gate_up[0]

time: 566 us -> 545 us (0.963)
  blocking collectives: 57.8 us -> 0 us
  starting transfers between devices: 8.24 us -> 30.4 us
  waiting for transfers between devices: 392 us -> 402 us
    all_gather x1 -> x0, waiting for transfers between devices: 96.6 us -> none  [per_device(): lax.all_gather(got_tok, 'dp', axis=0, tiled=True)]
    all_gather x1, waiting for transfers between devices: 68.2 us -> 148 us  [per_device(): lax.all_gather(got_cot, 'dp', axis=0, tiled=True)]
    all_to_all x2 -> x0, blocking collectives: 57.8 us -> none  [the longest x1 31.5 us: per_device(): lax.all_to_all(send_tok, 'expert', split_axis=0, concat_axis=0, tiled=True)]
    all_to_all x0 -> x3, waiting for transfers between devices: none -> 30.3 us  [the longest x1 15.4 us: per_device(): lax.all_to_all(send_tok, 'expert', split_axis=0, concat_axis=0, tiled=True)]
    all_to_all x0 -> x3, starting transfers between devices: none -> 22.2 us  [the longest x1 10 us: per_device(): lax.all_to_all(send_cot, 'expert', split_axis=0, concat_axis=0, tiled=True)]
  transfers between devices with their start and end apart: 4 -> 6, of which waited for: 4 -> 5; matrix products, arithmetic and copies ran while one was open for 4% -> 5% of each run, Pallas kernels for 0% -> 0%
where the time goes in v1:
time: 545 us; the launch traced here: 544 us
  waiting for transfers between devices  402 us (74%)
  local copies, waits for them, and re-layouts  53.1 us (10%)
  starting transfers between devices  30.4 us (6%)
  other arithmetic  22.7 us (4%)
  matrix products  20.3 us (4%)
  between operations  14.8 us (3%)
    reduce_scatter x1, waiting for transfers between devices, per_device(): lax.psum_scatter(partial_value, 'dp', scatter_dimension=0, tiled=True)  214 us
    all_gather x1, waiting for transfers between devices, per_device(): lax.all_gather(got_cot, 'dp', axis=0, tiled=True)  148 us
    all_to_all x1, waiting for transfers between devices, per_device(): lax.all_to_all(send_tok, 'expert', split_axis=0, concat_axis=0, tiled=True)  15.4 us
    all_to_all x1, waiting for transfers between devices, per_device(): lax.all_to_all(send_cot, 'expert', split_axis=0, concat_axis=0, tiled=True)  15 us
    dot_general x7, matrix products, contract(): lax.dot_general(left, right, (((left_dim,), (right_dim,)), ((), ())), pre...  14.4 us
    scatter x1, local copies, waits for them, and re-layouts, advance(): input_all = input_all.at[picked].set(input_rows)  11.1 us
  transfers between devices with their start and end apart: 6, of which 5 were waited for; matrix products, arithmetic and copies ran while one was open for 5% of the time, Pallas kernels for 0%

profile of v1, /device:TPU:1, one launch (start us, length us, event | category | flops | bytes accessed | tf_op | source)
XLA Modules:
  0.0 543.5 jit_solution(11456009413045295143)
XLA Ops:
  7.2 0.0 copy-start
  7.2 0.8 fusion.18
  8.0 0.2 reduce_window_sum.11
  8.2 0.8 select_reduce_fusion
  9.0 0.7 compare_select_fusion.1
  9.7 1.6 convolution_convert_fusion.2
  11.3 1.1 all_to_all.25
  12.5 10.0 %all-to-all-start = ((bf16[32,2,4096]{2,1,0:T(2,128)(2,1)}), bf16[32,2,4096]{2,1,0:T(2,128)(2,1)S(1)}, u32[]{:S(2)}, u32[]{:S(2)}) async-start(bf16[32,2,4096]{2,1,0:T(2,128)(2,1)} %all_to_all.25), calls=%async_computation | async-start | bytes 1048576 | tf_op jit(solution)/shard_map/all_to_all | solution.py:90
  22.5 0.0 copy-done
  22.5 0.3 convolution_convert_fusion.1
  22.8 1.1 all_to_all.28
  23.9 0.0 copy-done.9
  23.9 15.0 %all-to-all-done = bf16[32,2,4096]{2,1,0:T(2,128)(2,1)S(1)} async-done(((bf16[32,2,4096]{2,1,0:T(2,128)(2,1)}), bf16[32,2,4096]{2,1,0:T(2,128)(2,1)S(1)}, u32[]{:S(2)}, u32[]{:S(2)}) %all-to-all-start) | async-done | bytes 524320 | tf_op jit(solution)/shard_map/all_to_all | solution.py:90
  38.9 4.1 all-to-all-start.1
  43.0 0.0 all-gather.2.cloned.1.call-start
  43.0 1.0 all_to_all.27
  44.0 0.0 all-gather.2.cloned.1.call-update
  44.1 15.4 %all-to-all-done.1 = bf16[32,2,4096]{2,1,0:T(2,128)(2,1)S(1)} async-done(((bf16[32,2,4096]{2,1,0:T(2,128)(2,1)}), bf16[32,2,4096]{2,1,0:T(2,128)(2,1)S(1)}, u32[]{:S(2)}, u32[]{:S(2)}) %all-to-all-start.1) | async-done | bytes 524320 | tf_op jit(solution)/shard_map/all_to_all | solution.py:89
  59.4 0.2 stack.10
  59.6 2.5 stack.11
  62.1 8.1 %all-to-all-start.2 = ((bf16[8,64,4096]{2,1,0:T(8,128)(2,1)}), bf16[8,64,4096]{2,1,0:T(8,128)(2,1)}, u32[]{:S(2)}, u32[]{:S(2)}) async-start(bf16[8,64,4096]{2,1,0:T(8,128)(2,1)} %stack.11), calls=%async_computation.2 | async-start | bytes 8388608 | tf_op jit(solution)/shard_map/all_to_all | solution.py:11
  70.2 0.0 reduce-scatter.2.cloned.1.call-start
  70.3 6.0 %copy.9 = bf16[1,2,4096,192]{3,2,1,0:T(8,128)(2,1)} copy(bf16[1,2,4096,192]{2,3,1,0:T(8,128)(2,1)} %param.14) | data formatting | bytes 6291456 | tf_op args[4]
  76.3 147.6 %all-gather.2.cloned.1.call-done = bf16[512,4096]{1,0:T(8,128)(2,1)} async-done(((bf16[64,4096]{1,0:T(8,128)(2,1)}), bf16[512,4096]{1,0:T(8,128)(2,1)}) %all-gather.2.cloned.1.call-update) | async-done | bytes 4194320 | tf_op jit(solution)/shard_map/all_gather | solution.py:94
  223.9 3.3 compare_reduce_fusion
  227.2 0.6 convert_subtract_fusion
  228.5 3.8 sort.17
  232.3 0.0 all-to-all-done.2
  232.3 2.1 broadcast.33.clone
  234.4 2.1 broadcast_in_dim.28
  236.5 2.0 broadcast.33
  238.5 4.3 broadcast_in_dim.29
  242.8 46.4 %while.16 = (s32[]{:T(128)}, f32[4096,192]{0,1:T(8,128)}, f32[4096,192]{0,1:T(8,128)}, f32[192,4096]{1,0:T(8,128)}, f32[512,4096]{1,0:T(8,128)}, /*index=5*/s32[...) while((s32[]{:T(128)}, f32[4096,192]{0,1:T(8,128)}, ...), condition=%wide.region_7.9_spmd, body=%wide.region_5.8_spmd.sunk | while | flops 3231861248 | bytes 160641424 | solution.py:67
  242.8 0.1 compare_and_fusion.2
  242.8 6.6 %gather_fusion = bf16[256,4096]{1,0:T(8,128)(2,1)S(1)} fusion(bf16[512,4096]{1,0:T(8,128)(2,1)} %get-tuple-element.214, s32[1024]{0:T(1024)S(1)} %pad_clamp_fusion.2), kind=kCustom, calls=%fused_computation.clone.clone.1 | custom fusion | bytes 4195328 | tf_op jit(solution)/shard_map/while/body/jit(_take)/gather | solution.py:53
  249.5 2.8 fusion.51
  252.3 0.0 copy-done.7
  252.3 1.1 fusion.50
  253.4 7.9 %gather_fusion.1 = bf16[256,4096]{1,0:T(8,128)(2,1)} fusion(bf16[512,4096]{1,0:T(8,128)(2,1)} %get-tuple-element.215, s32[1024]{0:T(1024)S(1)} %pad_clamp_fusion.2), kind=kCustom, calls=%fused_computation.1.clone.clone.1 | custom fusion | bytes 4195328 | tf_op jit(solution)/shard_map/while/body/jit(_take)/gather | solution.py:54
  261.3 3.1 multiply_convert_fusion.9
  264.5 0.0 copy-start.5
  264.5 4.5 convolution_add_fusion.10
  269.0 0.9 convolution_add_fusion.8
  269.9 0.0 copy-start.6
  269.9 1.7 copy-done.6
  271.6 0.0 copy-done.3
  271.6 0.9 convolution_add_fusion.9
  272.5 1.7 copy-done.4
  274.2 0.3 copy-done.8
  274.5 0.8 fusion.52
  275.3 2.8 convolution_add_fusion.11
  278.1 11.1 %scatter_fusion = f32[512,4096]{1,0:T(8,128)} fusion(f32[512,4096]{1,0:T(8,128)} %get-tuple-element.196, s32[256]{0:T(256)S(1)} %get-tuple-element.173, f32[256,4096]{1,0:T(8,128)} %convolution_add_fusion.11), kind=kCustom, calls=%fused_computation.2.clone.1 | custom fusion | bytes 12583936 | tf_op jit(solution)/shard_map/while/body/scatter | solution.py:58
  289.2 0.0 reduce-scatter.2.cloned.1.call-update
  289.2 4.4 convert_bitcast_fusion.1
  293.7 214.4 %reduce-scatter.2.cloned.1.call-done = f32[64,4096]{1,0:T(8,128)} async-done(((f32[512,4096]{1,0:T(8,128)}), f32[64,4096]{1,0:T(8,128)}) %reduce-scatter.2.cloned.1.call-update) | async-done | bytes 1048592 | tf_op jit(solution)/shard_map/reduce_scatter | solution.py:99
  508.0 1.3 convert_element_type.55
  509.3 1.1 all_to_all.31
  510.5 8.1 %all-to-all-start.3 = ((bf16[32,2,4096]{2,1,0:T(2,128)(2,1)}), bf16[32,2,4096]{2,1,0:T(2,128)(2,1)S(1)}, u32[]{:S(2)}, u32[]{:S(2)}) async-start(bf16[32,2,4096]{2,1,0:T(2,128)(2,1)} %all_to_all.31), calls=%async_computation.4 | async-start | bytes 1048576 | tf_op jit(solution)/shard_map/all_to_all | solution.py:101
  518.6 3.4 pad_maximum_fusion
  522.0 3.3 convert_bitcast_fusion
  525.3 9.7 %all-to-all-done.3 = bf16[32,2,4096]{2,1,0:T(2,128)(2,1)S(1)} async-done(((bf16[32,2,4096]{2,1,0:T(2,128)(2,1)}), bf16[32,2,4096]{2,1,0:T(2,128)(2,1)S(1)}, u32[]{:S(2)}, u32[]{:S(2)}) %all-to-all-start.3) | async-done | bytes 524320 | tf_op jit(solution)/shard_map/all_to_all | solution.py:101
  535.0 0.2 all_to_all.33
  535.2 0.0 copy-done.10
  535.2 1.5 convolution_convert_fusion
  (13 shorter events, 0.0 us)
Async XLA Ops:
  7.2 15.3 %copy-start = (bf16[128,4096]{1,0:T(8,128)(2,1)S(1)}, bf16[128,4096]{1,0:T(8,128)(2,1)}, u32[]{:S(2)}) copy-start(bf16[128,4096]{1,0:T(8,128)(2,1)} %param.10) | copy-start | bytes 3145732
  9.7 14.2 %copy-start.9 = (s32[128]{0:T(128)}, s32[128]{0:T(128)S(1)}, u32[]{:S(2)}) copy-start(s32[128]{0:T(128)S(1)} %compare_select_fusion.1) | copy-start | bytes 1540
  12.5 26.4 %all-to-all-start = ((bf16[32,2,4096]{2,1,0:T(2,128)(2,1)}), bf16[32,2,4096]{2,1,0:T(2,128)(2,1)S(1)}, u32[]{:S(2)}, u32[]{:S(2)}) async-start(bf16[32,2,4096]{2,1,0:T(2,128)(2,1)} %all_to_all.25), calls=%async_computation | async-start | bytes 1048576 | tf_op jit(solution)/shard_map/all_to_all | solution.py:90
  38.9 20.5 %all-to-all-start.1 = ((bf16[32,2,4096]{2,1,0:T(2,128)(2,1)}), bf16[32,2,4096]{2,1,0:T(2,128)(2,1)S(1)}, u32[]{:S(2)}, u32[]{:S(2)}) async-start(bf16[32,2,4096]{2,1,0:T(2,128)(2,1)} %all_to_all.28), calls=%async_computation.1 | async-start | bytes 1048576 | tf_op jit(solution)/shard_map/all_to_all | solution.py:89
  43.0 180.9 %all-gather.2.cloned.1.call-start = ((), (), s32[]{:S(2)}) async-start(), calls=%async_computation.5 | async-start | bytes 4718592 | tf_op jit(solution)/shard_map/all_gather | solution.py:94
  62.1 170.2 %all-to-all-start.2 = ((bf16[8,64,4096]{2,1,0:T(8,128)(2,1)}), bf16[8,64,4096]{2,1,0:T(8,128)(2,1)}, u32[]{:S(2)}, u32[]{:S(2)}) async-start(bf16[8,64,4096]{2,1,0:T(8,128)(2,1)} %stack.11), calls=%async_computation.2 | async-start | bytes 8388608 | tf_op jit(solution)/shard_map/all_to_all | solution.py:11
  70.2 437.8 %reduce-scatter.2.cloned.1.call-start = ((), (), s32[]{:S(2)}) async-start(), calls=%async_computation.6 | async-start | bytes 9437184 | tf_op jit(solution)/shard_map/reduce_scatter | solution.py:99
  249.5 2.8 copy-start.7
  261.3 3.1 copy-start.2
  264.5 4.5 copy-start.5
  269.0 2.6 copy-start.3
  269.9 1.7 copy-start.6
  271.6 3.0 copy-start.8
  272.5 1.7 copy-start.4
  510.5 24.6 %all-to-all-start.3 = ((bf16[32,2,4096]{2,1,0:T(2,128)(2,1)}), bf16[32,2,4096]{2,1,0:T(2,128)(2,1)S(1)}, u32[]{:S(2)}, u32[]{:S(2)}) async-start(bf16[32,2,4096]{2,1,0:T(2,128)(2,1)} %all_to_all.31), calls=%async_computation.4 | async-start | bytes 1048576 | tf_op jit(solution)/shard_map/all_to_all | solution.py:101
  521.9 13.3 %copy-start.10 = (s32[128]{0:T(128)S(1)}, s32[128]{0:T(128)}, u32[]{:S(2)}) copy-start(s32[128]{0:T(128)} %copy-done.9) | copy-start | bytes 1540
  522.0 14.7 %copy-start.1 = (bf16[128,4096]{1,0:T(8,128)(2,1)S(1)}, bf16[128,4096]{1,0:T(8,128)(2,1)}, u32[]{:S(2)}) copy-start(bf16[128,4096]{1,0:T(8,128)(2,1)} %param.10) | copy-start | bytes 3145732
Sparse Core Ops, SparseCore 0:
  47.0 176.8 all-gather.1
  289.3 218.6 reduce-scatter.1
